TPU v7x, 32 devices: a whole 2x2x4 slice. The times are simulated.
32 devices in a mesh: lat: 4 (over y, x), lon: 8 (over z, core).
Axes of the slice: x: 2, y: 2, z: 4, core: 2. Of those that a mesh axis runs over, the one named last changes fastest.
Arguments:
- inputs: bfloat16 [360, 360, 256], P('lat', 'lon'), may hold values from -6 to 6
- kernel: bfloat16 [3, 3, 256, 256], replicated, may hold values from -0.125 to 0.125
- cotangent: bfloat16 [360, 360, 256], P('lat', 'lon'), may hold values from -6 to 6
Outputs:
- outputs: bfloat16 [360, 360, 256], P('lat', 'lon')
- input_grad: bfloat16 [360, 360, 256], P('lat', 'lon')
- kernel_grad: float32 [3, 3, 256, 256], replicated
All inputs are finite; a program needn't handle non-finite values.
Results may differ from a plain program's by a relative error of at most 0.001.
Values may be sent and summed in bfloat16 or wider, within the bound.
No kernel may reach another device: no remote copies, remote signals or barrier semaphores. Data moves between devices by JAX's collectives and lax.ppermute only.
A program may use at most 192 MiB of HBM per device.

v0:
```python
import math
import jax
import jax.numpy as jnp
from jax import lax
from jax.sharding import PartitionSpec as P


def with_halo(cells, sides, width):
    for axis, dim in sides:
        count = lax.axis_size(axis)
        head = lax.slice_in_dim(cells, 0, width, axis=dim)
        tail = lax.slice_in_dim(cells, cells.shape[dim] - width, cells.shape[dim], axis=dim)
        cells = jnp.concatenate(
            [
                lax.ppermute(tail, axis, [(i, (i + 1) % count) for i in range(count)]),
                cells,
                lax.ppermute(head, axis, [((i + 1) % count, i) for i in range(count)]),
            ],
            axis=dim,
        )
    return cells


def from_behind(value, axis, steps):
    count = lax.axis_size(axis)
    pairs = [(source, (source + steps) % count) for source in range(count)]
    return lax.ppermute(value, axis, pairs)


def patches(padded, rows, cols):
    pieces = [
        padded[row_tap : row_tap + rows, col_tap : col_tap + cols]
        for row_tap in range(3)
        for col_tap in range(3)
    ]
    return jnp.concatenate(pieces, axis=-1).reshape(rows * cols, -1)


def surround(field):
    return with_halo(field, (("lat", 0), ("lon", 1)), 1)


def polar(padded):
    both = jnp.stack([padded[1], padded[-2]])
    moved = from_behind(both, "lon", lax.axis_size("lon") // 2)
    return (moved[0], moved[1])


def edge_term(row_data, weights, cols, width):
    stacked = jnp.concatenate([row_data[offset : offset + cols] for offset in range(3)], axis=-1)
    return jnp.dot(stacked, weights.reshape(-1, width), preferred_element_type=jnp.float32)


def local(inputs, kernel, cotangent):
    rows, cols, width = inputs.shape
    north = lax.axis_index("lat") == 0
    south = lax.axis_index("lat") == lax.axis_size("lat") - 1
    padded = surround(inputs)
    top, bottom = polar(padded)
    padded = jnp.concatenate(
        [
            jnp.where(north, top, padded[0])[None],
            padded[1:-1],
            jnp.where(south, bottom, padded[-1])[None],
        ],
        0,
    )
    columns = patches(padded, rows, cols)
    outputs = jnp.dot(columns, kernel.reshape(-1, width), preferred_element_type=jnp.float32)
    outputs = outputs.reshape(rows, cols, width).astype(jnp.bfloat16)
    flat_grad = cotangent.reshape(-1, width)
    local_grad = lax.dot_general(
        columns, flat_grad, (((0,), (0,)), ((), ())), preferred_element_type=jnp.float32
    )
    local_grad = local_grad.reshape(3, 3, width, width)
    padded_grad = surround(cotangent)
    grad_top, grad_bottom = polar(padded_grad)
    empty_row = jnp.zeros_like(padded_grad[0])
    padded_grad = jnp.concatenate(
        [
            jnp.where(north, empty_row, padded_grad[0])[None],
            padded_grad[1:-1],
            jnp.where(south, empty_row, padded_grad[-1])[None],
        ],
        0,
    )
    flipped = jnp.transpose(kernel[::-1, ::-1], (0, 1, 3, 2))
    input_grad = jnp.dot(
        patches(padded_grad, rows, cols),
        flipped.reshape(-1, width),
        preferred_element_type=jnp.float32,
    )
    input_grad = input_grad.reshape(rows, cols, width)
    north_term = edge_term(grad_top, flipped[2], cols, width)
    south_term = edge_term(grad_bottom, flipped[0], cols, width)
    input_grad = input_grad.at[0].add(jnp.where(north, north_term, 0.0))
    input_grad = input_grad.at[-1].add(jnp.where(south, south_term, 0.0))
    factor = 1.0 / math.sqrt(rows * cols * lax.axis_size("lat") * lax.axis_size("lon"))
    partial_sum = lax.psum(local_grad, "lon")
    summed = lax.psum(partial_sum, "lat")
    return (outputs, input_grad.astype(jnp.bfloat16), summed * factor)


def solution(mesh):
    in_specs = (P("lat", "lon", None), P(), P("lat", "lon", None))
    out_specs = (P("lat", "lon", None), P("lat", "lon", None), P())
    return jax.shard_map(local, mesh=mesh, in_specs=in_specs, out_specs=out_specs, check_vma=False)
```

profile of v0, /device:TPU:0, one launch (start us, length us, event | category | flops | bytes accessed | tf_op | source)
XLA Modules:
  0.0 271.3 jit_solution(15557798716294932809)
XLA Ops:
  8.0 3.9 %collective-permute-start.1 = (bf16[1,45,256]{2,1,0:T(8,128)(2,1)S(1)}, bf16[1,45,256]{2,1,0:T(8,128)(2,1)S(1)}, u32[]{:S(2)}, u32[]{:S(2)}) collective-permute-start(bf16[1,45,256]{2,1,0:T(8,128)(2,1)S(1)} %get-tuple-element.37), channel_id=1, source_target_pairs={{8,0},{16,8},{24,16},{0,24},{9,1},{17,9},{25,17},{1,25},{10,2},{18... | collective-permute-start | bytes 69128 | tf_op jit(solution)/shard_map/ppermute | solution.py:17
  13.3 2.9 %collective-permute-start.6 = (bf16[1,45,256]{2,1,0:T(8,128)(2,1)}, bf16[1,45,256]{2,1,0:T(8,128)(2,1)S(1)}, u32[]{:S(2)}, u32[]{:S(2)}) collective-permute-start(bf16[1,45,256]{2,1,0:T(8,128)(2,1)} %get-tuple-element.35), channel_id=1, source_target_pairs={{8,0},{16,8},{24,16},{0,24},{9,1},{17,9},{25,17},{1,25},{10,2},{18... | collective-permute-start | bytes 69128 | tf_op jit(solution)/shard_map/ppermute | solution.py:17
  19.9 1.9 reshape.103
  22.2 3.5 %collective-permute-start.8 = (bf16[92,1,256]{2,1,0:T(2,128)(2,1)S(1)}, bf16[92,1,256]{2,1,0:T(2,128)(2,1)S(1)}, u32[]{:S(2)}, u32[]{:S(2)}) collective-permute-start(bf16[92,1,256]{2,1,0:T(2,128)(2,1)S(1)} %get-tuple-element.32), channel_id=1, source_target_pairs={{1,0},{2,1},{3,2},{4,3},{5,4},{6,5},{7,6},{0,7},{9,8},{10,9},{11,1... | collective-permute-start | bytes 141320 | tf_op jit(solution)/shard_map/ppermute | solution.py:17
  26.2 3.5 %collective-permute-start.3 = (bf16[92,1,256]{2,1,0:T(2,128)(2,1)S(1)}, bf16[92,1,256]{2,1,0:T(2,128)(2,1)S(1)}, u32[]{:S(2)}, u32[]{:S(2)}) collective-permute-start(bf16[92,1,256]{2,1,0:T(2,128)(2,1)S(1)} %get-tuple-element.34), channel_id=1, source_target_pairs={{1,0},{2,1},{3,2},{4,3},{5,4},{6,5},{7,6},{0,7},{9,8},{10,9},{11,1... | collective-permute-start | bytes 141320 | tf_op jit(solution)/shard_map/ppermute | solution.py:17
  29.8 2.6 collective-permute-done.2
  34.6 1.6 fusion.7
  36.2 2.8 %fusion.5 = bf16[90,45,2304]{2,1,0:T(8,128)(2,1)} fusion(bf16[90,45,2304]{2,1,0:T(8,128)(2,1)} %fusion.7, bf16[1,47,256]{2,1,0:T(8,128)(2,1)S(1)} %get-tuple-element.30, bf16[90,47,256]{2,1,0:T(8,128)(2,1)S(1)} %slice.295), kind=kLoop, calls=%fused_computation.15 | loop fusion | flops 4147200 | bytes 4401664
  40.7 1.7 fusion.15
  42.5 2.7 %fusion.13 = bf16[90,45,2304]{2,1,0:T(8,128)(2,1)} fusion(bf16[90,45,2304]{2,1,0:T(8,128)(2,1)} %fusion.15, bf16[1,47,256]{2,1,0:T(8,128)(2,1)S(1)} %get-tuple-element.28, bf16[90,47,256]{2,1,0:T(8,128)(2,1)S(1)} %slice.283), kind=kLoop, calls=%fused_computation.23 | loop fusion | flops 4147200 | bytes 4401664
  45.2 2.8 %fusion.23 = bf16[90,45,2304]{2,1,0:T(8,128)(2,1)} fusion(bf16[90,45,2304]{2,1,0:T(8,128)(2,1)} %fusion.13, bf16[90,47,256]{2,1,0:T(8,128)(2,1)S(1)} %slice.283, bf16[1,47,256]{2,1,0:T(8,128)(2,1)S(1)} %get-tuple-element.28), kind=kLoop, calls=%fused_computation.41 | loop fusion | flops 4147200 | bytes 4401664
  48.0 2.9 %fusion.22 = bf16[90,45,2304]{2,1,0:T(8,128)(2,1)} fusion(bf16[90,45,2304]{2,1,0:T(8,128)(2,1)} %fusion.23, bf16[92,45,256]{2,1,0:T(8,128)(2,1)S(1)} %constant_dynamic-update-slice_fusion, bf16[92,1,256]{2,1,0:T(2,128)(2,1)S(1)} %collective-permute-done.2), kind=kLoop, calls=%fused_computation.39 | loop fusion | flops 4147200 | bytes 4378624
  50.8 1.7 constant_dynamic-update-slice_fusion.3
  52.5 3.1 %fusion.21 = bf16[90,45,2304]{2,1,0:T(8,128)(2,1)} fusion(bf16[90,45,2304]{2,1,0:T(8,128)(2,1)} %constant_dynamic-update-slice_fusion.3, bf16[92,1,256]{2,1,0:T(2,128)(2,1)S(1)} %collective-permute-done.3, bf16[92,45,256]{2,1,0:T(8,128)(2,1)S(1)} %constant_dynamic-update-slice_fusion), kind=kLoop, calls=%fused_computation.37 | loop fusion | flops 4147200 | bytes 4378624
  55.6 1.7 fusion.11
  57.3 2.8 %fusion.9 = bf16[90,45,2304]{2,1,0:T(8,128)(2,1)} fusion(bf16[90,45,2304]{2,1,0:T(8,128)(2,1)} %fusion.11, bf16[1,47,256]{2,1,0:T(8,128)(2,1)S(1)} %get-tuple-element.27, bf16[90,47,256]{2,1,0:T(8,128)(2,1)S(1)} %slice.283), kind=kLoop, calls=%fused_computation.19 | loop fusion | flops 4147200 | bytes 4401664
  60.0 3.1 %fusion.20 = bf16[90,45,2304]{2,1,0:T(8,128)(2,1)} fusion(bf16[90,45,2304]{2,1,0:T(8,128)(2,1)} %fusion.9, bf16[1,47,256]{2,1,0:T(8,128)(2,1)S(1)} %get-tuple-element.27, bf16[90,47,256]{2,1,0:T(8,128)(2,1)S(1)} %slice.283), kind=kLoop, calls=%fused_computation.35 | loop fusion | flops 4147200 | bytes 4401664 | tf_op jit(solution)/shard_map/concatenate | solution.py:36
  63.2 19.5 %reshape.99 = bf16[4050,2304]{1,0:T(8,128)(2,1)} reshape(bf16[90,45,2304]{2,1,0:T(8,128)(2,1)} %fusion.20) | data formatting | bytes 37324800 | tf_op jit(solution)/shard_map/reshape | solution.py:36
  82.7 23.0 %copy.7 = bf16[4050,2304]{0,1:T(8,128)(2,1)} copy(bf16[4050,2304]{1,0:T(8,128)(2,1)} %reshape.99) | data formatting | bytes 37324800 | tf_op jit(solution)/shard_map/reshape | solution.py:36
  105.7 10.6 %fusion.24 = f32[3,3,256,256]{3,2,1,0:T(8,128)} fusion(bf16[3,3,256,4050]{3,2,1,0:T(8,128)(2,1)} %bitcast.46, bf16[4050,256,1,1]{1,0,2,3:T(8,128)(2,1)} %reshape.103), kind=kOutput, calls=%fused_computation.42 | convolution fusion | flops 4777574400 | bytes 23095296 | tf_op jit(solution)/shard_map/dot_general | solution.py:72
  116.4 2.7 fusion.19
  119.1 2.8 %fusion.18 = bf16[90,45,2304]{2,1,0:T(8,128)(2,1)} fusion(bf16[90,45,2304]{2,1,0:T(8,128)(2,1)} %fusion.19, bf16[92,45,256]{2,1,0:T(8,128)(2,1)S(1)} %copy-done.1, bf16[92,1,256]{2,1,0:T(2,128)(2,1)S(1)} %collective-permute-done.7), kind=kLoop, calls=%fused_computation.31 | loop fusion | flops 4147200 | bytes 4378624
  121.9 1.6 constant_dynamic-update-slice_fusion.7
  123.4 2.9 %fusion.17 = bf16[90,45,2304]{2,1,0:T(8,128)(2,1)} fusion(bf16[90,45,2304]{2,1,0:T(8,128)(2,1)} %constant_dynamic-update-slice_fusion.7, bf16[92,1,256]{2,1,0:T(2,128)(2,1)S(1)} %collective-permute-done.8, bf16[92,45,256]{2,1,0:T(8,128)(2,1)S(1)} %copy-done.1), kind=kLoop, calls=%fused_computation.29 | loop fusion | flops 4147200 | bytes 4378624
  127.9 2.7 %fusion.1 = bf16[90,45,2304]{2,1,0:T(8,128)(2,1)} fusion(bf16[90,45,2304]{2,1,0:T(8,128)(2,1)} %fusion.3, bf16[1,47,256]{2,1,0:T(8,128)(2,1)S(1)} %get-tuple-element.29, bf16[90,47,256]{2,1,0:T(8,128)(2,1)S(1)} %slice.295), kind=kLoop, calls=%fused_computation.11 | loop fusion | flops 4147200 | bytes 4401664
  130.7 2.7 fusion.16
  133.4 51.7 %all-reduce.3.cloned.1.call-done = f32[3,3,256,256]{3,2,1,0:T(8,128)} async-done(((f32[3,3,256,256]{3,2,1,0:T(8,128)}), f32[3,3,256,256]{3,2,1,0:T(8,128)}) %all-reduce.3.cloned.1.call-update) | async-done | bytes 2359312 | tf_op jit(solution)/shard_map/psum | solution.py:99
  185.2 9.9 %fusion.72 = f32[90,45,256]{2,1,0:T(8,128)S(1)} fusion(bf16[90,45,2304]{2,1,0:T(8,128)(2,1)} %fusion.16, bf16[2304,256,1]{1,0,2:T(8,128)(2,1)S(1)} %bitcast.50), kind=kOutput, calls=%fused_computation.114 | convolution fusion | flops 4777574400 | bytes 23989248 | tf_op jit(solution)/shard_map/dot_general | solution.py:88
  195.6 1.6 convert_element_type.7
  197.2 11.6 %convolution_convert_fusion = bf16[90,45,256]{2,1,0:T(8,128)(2,1)} fusion(bf16[90,45,2304]{2,1,0:T(8,128)(2,1)} %fusion.20, bf16[2304,256,1]{1,0,2:T(8,128)(2,1)S(1)} %bitcast.49), kind=kOutput, calls=%fused_computation.44 | convolution fusion | flops 4778611200 | bytes 21915648 | tf_op jit(solution)/shard_map/dot_general | solution.py:69
  208.8 52.4 %all-reduce.5.cloned.1.call-done = f32[3,3,256,256]{3,2,1,0:T(8,128)} async-done(((f32[3,3,256,256]{3,2,1,0:T(8,128)}), f32[3,3,256,256]{3,2,1,0:T(8,128)}) %all-reduce.5.cloned.1.call-update) | async-done | bytes 2359312 | tf_op jit(solution)/shard_map/psum | solution.py:100
  261.2 3.3 %broadcast_multiply_fusion = f32[3,3,256,256]{3,2,1,0:T(8,128)} fusion(f32[3,3,256,256]{3,2,1,0:T(8,128)} %all-reduce.5.cloned.1.call-done), kind=kLoop, calls=%fused_computation.45 | loop fusion | flops 589824 | bytes 4718592 | tf_op jit(solution)/shard_map/mul | solution.py:101
  (63 shorter events, 12.7 us)
Async XLA Ops:
  7.2 178.0 %all-reduce.3.cloned.1.call-start = ((), (), s32[]{:S(2)}) async-start(), calls=%async_computation | async-start | bytes 4718592 | tf_op jit(solution)/shard_map/psum | solution.py:99
  8.0 18.0 %collective-permute-start.1 = (bf16[1,45,256]{2,1,0:T(8,128)(2,1)S(1)}, bf16[1,45,256]{2,1,0:T(8,128)(2,1)S(1)}, u32[]{:S(2)}, u32[]{:S(2)}) collective-permute-start(bf16[1,45,256]{2,1,0:T(8,128)(2,1)S(1)} %get-tuple-element.37), channel_id=1, source_target_pairs={{8,0},{16,8},{24,16},{0,24},{9,1},{17,9},{25,17},{1,25},{10,2},{18... | collective-permute-start | bytes 69128 | tf_op jit(solution)/shard_map/ppermute | solution.py:17
  11.9 13.9 %collective-permute-start = (bf16[1,45,256]{2,1,0:T(8,128)(2,1)S(1)}, bf16[1,45,256]{2,1,0:T(8,128)(2,1)S(1)}, u32[]{:S(2)}, u32[]{:S(2)}) collective-permute-start(bf16[1,45,256]{2,1,0:T(8,128)(2,1)S(1)} %get-tuple-element.38), channel_id=1, source_target_pairs={{0,8},{8,16},{16,24},{24,0},{1,9},{9,17},{17,25},{25,1},{2,10},{10... | collective-permute-start | bytes 69128 | tf_op jit(solution)/shard_map/ppermute | solution.py:15
  13.3 8.7 %collective-permute-start.6 = (bf16[1,45,256]{2,1,0:T(8,128)(2,1)}, bf16[1,45,256]{2,1,0:T(8,128)(2,1)S(1)}, u32[]{:S(2)}, u32[]{:S(2)}) collective-permute-start(bf16[1,45,256]{2,1,0:T(8,128)(2,1)} %get-tuple-element.35), channel_id=1, source_target_pairs={{8,0},{16,8},{24,16},{0,24},{9,1},{17,9},{25,17},{1,25},{10,2},{18... | collective-permute-start | bytes 69128 | tf_op jit(solution)/shard_map/ppermute | solution.py:17
  16.2 5.6 %collective-permute-start.5 = (bf16[1,45,256]{2,1,0:T(8,128)(2,1)}, bf16[1,45,256]{2,1,0:T(8,128)(2,1)S(1)}, u32[]{:S(2)}, u32[]{:S(2)}) collective-permute-start(bf16[1,45,256]{2,1,0:T(8,128)(2,1)} %get-tuple-element.36), channel_id=1, source_target_pairs={{0,8},{8,16},{16,24},{24,0},{1,9},{9,17},{17,25},{25,1},{2,10},{10... | collective-permute-start | bytes 69128 | tf_op jit(solution)/shard_map/ppermute | solution.py:15
  17.9 2.0 copy-start.2
  21.8 4.0 %copy-start.4 = (bf16[90,45,256]{2,1,0:T(8,128)(2,1)S(1)}, bf16[90,45,256]{2,1,0:T(8,128)(2,1)}, u32[]{:S(2)}) copy-start(bf16[90,45,256]{2,1,0:T(8,128)(2,1)} %param.7) | copy-start | bytes 6220804
  22.0 12.5 %copy-start = (bf16[92,45,256]{2,1,0:T(8,128)(2,1)}, bf16[92,45,256]{2,1,0:T(8,128)(2,1)S(1)}, u32[]{:S(2)}) copy-start(bf16[92,45,256]{2,1,0:T(8,128)(2,1)S(1)} %constant_dynamic-update-slice_fusion.4) | copy-start | bytes 6359044
  22.2 7.5 %collective-permute-start.7 = (bf16[92,1,256]{2,1,0:T(2,128)(2,1)S(1)}, bf16[92,1,256]{2,1,0:T(2,128)(2,1)S(1)}, u32[]{:S(2)}, u32[]{:S(2)}) collective-permute-start(bf16[92,1,256]{2,1,0:T(2,128)(2,1)S(1)} %get-tuple-element.31), channel_id=1, source_target_pairs={{0,1},{1,2},{2,3},{3,4},{4,5},{5,6},{6,7},{7,0},{8,9},{9,10},{10,1... | collective-permute-start | bytes 141320 | tf_op jit(solution)/shard_map/ppermute | solution.py:15
  22.2 7.5 %collective-permute-start.8 = (bf16[92,1,256]{2,1,0:T(2,128)(2,1)S(1)}, bf16[92,1,256]{2,1,0:T(2,128)(2,1)S(1)}, u32[]{:S(2)}, u32[]{:S(2)}) collective-permute-start(bf16[92,1,256]{2,1,0:T(2,128)(2,1)S(1)} %get-tuple-element.32), channel_id=1, source_target_pairs={{1,0},{2,1},{3,2},{4,3},{5,4},{6,5},{7,6},{0,7},{9,8},{10,9},{11,1... | collective-permute-start | bytes 141320 | tf_op jit(solution)/shard_map/ppermute | solution.py:17
  26.1 6.3 %collective-permute-start.2 = (bf16[92,1,256]{2,1,0:T(2,128)(2,1)S(1)}, bf16[92,1,256]{2,1,0:T(2,128)(2,1)S(1)}, u32[]{:S(2)}, u32[]{:S(2)}) collective-permute-start(bf16[92,1,256]{2,1,0:T(2,128)(2,1)S(1)} %get-tuple-element.33), channel_id=1, source_target_pairs={{0,1},{1,2},{2,3},{3,4},{4,5},{5,6},{6,7},{7,0},{8,9},{9,10},{10,1... | collective-permute-start | bytes 141320 | tf_op jit(solution)/shard_map/ppermute | solution.py:15
  26.2 6.2 %collective-permute-start.3 = (bf16[92,1,256]{2,1,0:T(2,128)(2,1)S(1)}, bf16[92,1,256]{2,1,0:T(2,128)(2,1)S(1)}, u32[]{:S(2)}, u32[]{:S(2)}) collective-permute-start(bf16[92,1,256]{2,1,0:T(2,128)(2,1)S(1)} %get-tuple-element.34), channel_id=1, source_target_pairs={{1,0},{2,1},{3,2},{4,3},{5,4},{6,5},{7,6},{0,7},{9,8},{10,9},{11,1... | collective-permute-start | bytes 141320 | tf_op jit(solution)/shard_map/ppermute | solution.py:17
  29.8 165.3 %collective-permute-start.9 = (bf16[2,47,256]{2,1,0:T(8,128)(2,1)S(1)}, bf16[2,47,256]{2,1,0:T(8,128)(2,1)S(1)}, u32[]{:S(2)}, u32[]{:S(2)}) collective-permute-start(bf16[2,47,256]{2,1,0:T(8,128)(2,1)S(1)} %fusion.57), channel_id=1, source_target_pairs={{0,4},{1,5},{2,6},{3,7},{4,0},{5,1},{6,2},{7,3},{8,12},{9,13},{10,... | collective-permute-start | bytes 144392 | tf_op jit(solution)/shard_map/ppermute | solution.py:27
  32.4 8.3 %collective-permute-start.4 = (bf16[2,47,256]{2,1,0:T(8,128)(2,1)S(1)}, bf16[2,47,256]{2,1,0:T(8,128)(2,1)S(1)}, u32[]{:S(2)}, u32[]{:S(2)}) collective-permute-start(bf16[2,47,256]{2,1,0:T(8,128)(2,1)S(1)} %fusion.54), channel_id=1, source_target_pairs={{0,4},{1,5},{2,6},{3,7},{4,0},{5,1},{6,2},{7,3},{8,12},{9,13},{10,... | collective-permute-start | bytes 144392 | tf_op jit(solution)/shard_map/ppermute | solution.py:27
  116.3 144.9 %all-reduce.5.cloned.1.call-start = ((), (), s32[]{:S(2)}) async-start(), calls=%async_computation.1 | async-start | bytes 4718592 | tf_op jit(solution)/shard_map/psum | solution.py:100
  116.4 2.7 %copy-start.1 = (bf16[92,45,256]{2,1,0:T(8,128)(2,1)S(1)}, bf16[92,45,256]{2,1,0:T(8,128)(2,1)}, u32[]{:S(2)}) copy-start(bf16[92,45,256]{2,1,0:T(8,128)(2,1)} %copy-done) | copy-start | bytes 6359044
  119.1 2.8 %copy-start.3 = (bf16[90,45,256]{2,1,0:T(8,128)(2,1)S(1)}, bf16[90,45,256]{2,1,0:T(8,128)(2,1)}, u32[]{:S(2)}) copy-start(bf16[90,45,256]{2,1,0:T(8,128)(2,1)} %param.9) | copy-start | bytes 6220804
  133.4 51.8 %copy-start.8 = (bf16[3,3,256,256]{2,3,1,0:T(8,128)(2,1)S(1)}, bf16[3,3,256,256]{2,3,1,0:T(8,128)(2,1)}, u32[]{:S(2)}) copy-start(bf16[3,3,256,256]{2,3,1,0:T(8,128)(2,1)} %rev.3) | copy-start | bytes 3538948
  185.2 9.9 %copy-start.6 = (bf16[1,3,256,256]{3,2,1,0:T(8,128)(2,1)S(1)}, bf16[1,3,256,256]{3,2,1,0:T(8,128)(2,1)}, u32[]{:S(2)}) copy-start(bf16[1,3,256,256]{3,2,1,0:T(8,128)(2,1)} %get-tuple-element.40) | copy-start | bytes 1179652
  185.2 10.2 %copy-start.5 = (bf16[1,3,256,256]{3,2,1,0:T(8,128)(2,1)S(1)}, bf16[1,3,256,256]{3,2,1,0:T(8,128)(2,1)}, u32[]{:S(2)}) copy-start(bf16[1,3,256,256]{3,2,1,0:T(8,128)(2,1)} %get-tuple-element.39) | copy-start | bytes 1179652
  195.5 1.6 copy-start.7
Sparse Core Ops, SparseCore 0:
  116.4 68.6 all-reduce.2
  188.3 72.8 all-reduce.4
where the time goes:
time: 272 us; the launch traced here: 271 us
  waiting for transfers between devices  107 us (39%)
  local copies, waits for them, and re-layouts  54.5 us (20%)
  other arithmetic  48.6 us (18%)
  matrix products  32.5 us (12%)
  starting transfers between devices  14.6 us (5%)
  between operations  14.3 us (5%)
    psum x1, waiting for transfers between devices, local(): summed = lax.psum(partial_sum, 'lat')  52.4 us
    psum x1, waiting for transfers between devices, local(): partial_sum = lax.psum(local_grad, 'lon')  51.7 us
    reshape x2, local copies, waits for them, and re-layouts, patches(): return jnp.concatenate(pieces, axis=-1).reshape(rows * cols, -1)  42.5 us
    unnamed x14, other arithmetic  34.7 us
    ppermute x4, starting transfers between devices, with_halo(): lax.ppermute(head, axis, [((i + 1) % count, i) for i in range(count)])  13.9 us
    dot_general x1, matrix products, local(): jnp.dot(columns, kernel.reshape(-1, width), preferred_element_type=jnp.fl...  11.6 us
    dot_general x1, matrix products, local(): lax.dot_general(columns, flat_grad, (((0,), (0,)), ((), ())), preferred_e...  10.6 us
    dot_general x1, matrix products, local(): jnp.dot(patches(padded_grad, rows, cols), flipped.reshape(-1, width), pre...  9.87 us
  transfers between devices with their start and end apart: 12, of which 3 were waited for; matrix products, arithmetic and copies ran while one was open for 48% of the time, Pallas kernels for 0%

commit v1 on v0

--- a/solution.py
+++ b/solution.py
@@ -96,7 +96,8 @@
     input_grad = input_grad.at[0].add(jnp.where(north, north_term, 0.0))
     input_grad = input_grad.at[-1].add(jnp.where(south, south_term, 0.0))
     factor = 1.0 / math.sqrt(rows * cols * lax.axis_size("lat") * lax.axis_size("lon"))
-    partial_sum = lax.psum(local_grad, "lon")
+    choose_bench = lambda shard_in: lax.all_gather(shard_in, axis_name="lon").sum(axis=0)
+    partial_sum = choose_bench(local_grad)
     summed = lax.psum(partial_sum, "lat")
     return (outputs, input_grad.astype(jnp.bfloat16), summed * factor)
 

time: 272 us -> 369 us (1.36)
  waiting for transfers between devices: 107 us -> 178 us
  other arithmetic: 48.6 us -> 60.8 us
  local copies, waits for them, and re-layouts: 54.5 us -> 62 us
  starting transfers between devices: 14.6 us -> 20 us
    all_gather x0 -> x1, waiting for transfers between devices: none -> 121 us  [local(): lax.all_gather(shard_in, axis_name='lon').sum(axis=0)]
    psum x1 -> x0, waiting for transfers between devices: 51.7 us -> none  [local(): partial_sum = lax.psum(local_grad, 'lon')]
    reduce_sum x0 -> x1, other arithmetic: none -> 9.35 us  [local(): lax.all_gather(shard_in, axis_name='lon').sum(axis=0)]
    psum x1, waiting for transfers between devices: 52.4 us -> 45.9 us  [local(): summed = lax.psum(partial_sum, 'lat')]
    ppermute x4, waiting for transfers between devices: 2.58 us -> 9.04 us  [with_halo(): lax.ppermute(tail, axis, [(i, (i + 1) % count) for i in range(count)])]
    ppermute x2, starting transfers between devices: 0.48 us -> 6.79 us  [from_behind(): return lax.ppermute(value, axis, pairs)]
    unnamed x25 -> x23, local copies, waits for them, and re-layouts: 5.17 us -> 9.12 us
    ppermute x4, starting transfers between devices: 13.9 us -> 9.99 us  [with_halo(): lax.ppermute(head, axis, [((i + 1) % count, i) for i in range(count)])]
  transfers between devices with their start and end apart: 12 -> 12, of which waited for: 3 -> 6; matrix products, arithmetic and copies ran while one was open for 48% -> 20% of each run, Pallas kernels for 0% -> 0%
where the time goes in v1:
time: 369 us; the launch traced here: 368 us
  waiting for transfers between devices  178 us (48%)
  local copies, waits for them, and re-layouts  62 us (17%)
  other arithmetic  60.8 us (16%)
  matrix products  32.8 us (9%)
  starting transfers between devices  20 us (5%)
  between operations  14.2 us (4%)
    all_gather x1, waiting for transfers between devices, local(): lax.all_gather(shard_in, axis_name='lon').sum(axis=0)  121 us
    psum x1, waiting for transfers between devices, local(): summed = lax.psum(partial_sum, 'lat')  45.9 us
    reshape x2, local copies, waits for them, and re-layouts, patches(): return jnp.concatenate(pieces, axis=-1).reshape(rows * cols, -1)  43.8 us
    unnamed x14, other arithmetic  35.7 us
    dot_general x1, matrix products, local(): jnp.dot(columns, kernel.reshape(-1, width), preferred_element_type=jnp.fl...  11.6 us
    dot_general x1, matrix products, local(): jnp.dot(patches(padded_grad, rows, cols), flipped.reshape(-1, width), pre...  10.5 us
    dot_general x1, matrix products, local(): lax.dot_general(columns, flat_grad, (((0,), (0,)), ((), ())), preferred_e...  10.4 us
    ppermute x4, starting transfers between devices, with_halo(): lax.ppermute(head, axis, [((i + 1) % count, i) for i in range(count)])  9.99 us
  transfers between devices with their start and end apart: 12, of which 6 were waited for; matrix products, arithmetic and copies ran while one was open for 20% of the time, Pallas kernels for 0%

profile of v1, /device:TPU:0, one launch (start us, length us, event | category | flops | bytes accessed | tf_op | source)
XLA Modules:
  0.0 367.8 jit_solution(15508358272657188416)
XLA Ops:
  8.0 3.0 collective-permute-start
  15.7 3.5 collective-permute-start.3
  19.2 4.0 %reshape.109 = bf16[4050,256,1,1]{1,0,2,3:T(8,128)(2,1)} reshape(bf16[90,45,256]{2,1,0:T(8,128)(2,1)} %param.9) | data formatting | bytes 4147200 | tf_op jit(solution)/shard_map/reshape | solution.py:71
  26.4 2.3 collective-permute-done.4
  30.4 2.8 fusion.13
  33.2 2.8 fusion.23
  36.0 2.9 fusion.22
  40.6 2.9 fusion.21
  45.3 2.9 fusion.9
  48.2 2.7 fusion.20
  50.9 19.3 %reshape.103 = bf16[4050,2304]{1,0:T(8,128)(2,1)} reshape(bf16[90,45,2304]{2,1,0:T(8,128)(2,1)} %fusion.20) | data formatting | bytes 37324800 | tf_op jit(solution)/shard_map/reshape | solution.py:36
  70.3 24.5 %copy.10 = bf16[4050,2304]{0,1:T(8,128)(2,1)} copy(bf16[4050,2304]{1,0:T(8,128)(2,1)} %reshape.103) | data formatting | bytes 37324800 | tf_op jit(solution)/shard_map/reshape | solution.py:36
  94.7 10.4 %fusion.24 = f32[3,3,256,256]{3,2,1,0:T(8,128)} fusion(bf16[3,3,256,4050]{3,2,1,0:T(8,128)(2,1)} %bitcast.48, bf16[4050,256,1,1]{1,0,2,3:T(8,128)(2,1)S(1)} %copy-done.2), kind=kOutput, calls=%fused_computation.42 | convolution fusion | flops 4777574400 | bytes 23095296 | tf_op jit(solution)/shard_map/dot_general | solution.py:72
  106.0 1.9 collective-permute-start.6
  108.9 3.8 %collective-permute-done.5 = bf16[1,45,256]{2,1,0:T(8,128)(2,1)S(1)} collective-permute-done((bf16[1,45,256]{2,1,0:T(8,128)(2,1)S(1)}, bf16[1,45,256]{2,1,0:T(8,128)(2,1)S(1)}, u32[]{:S(2)}, u32[]{:S(2)}) %collective-permute-start.5) | collective-permute-done | bytes 23072 | tf_op jit(solution)/shard_map/ppermute | solution.py:15
  112.7 2.1 constant_dynamic-update-slice_fusion.5
  115.7 3.5 collective-permute-start.8
  121.3 3.5 collective-permute-done.7
  125.4 5.3 %collective-permute-start.9 = (bf16[2,47,256]{2,1,0:T(8,128)(2,1)S(1)}, bf16[2,47,256]{2,1,0:T(8,128)(2,1)S(1)}, u32[]{:S(2)}, u32[]{:S(2)}) collective-permute-start(bf16[2,47,256]{2,1,0:T(8,128)(2,1)S(1)} %fusion.57), channel_id=1, source_target_pairs={{0,4},{1,5},{2,6},{3,7},{4,0},{5,1},{6,2},{7,3},{8,12},{9,13},{10,... | collective-permute-start | bytes 144392 | tf_op jit(solution)/shard_map/ppermute | solution.py:27
  130.8 2.3 pad_maximum_fusion.1
  135.5 2.7 fusion.5
  138.3 2.8 fusion.19
  141.0 3.6 fusion.18
  146.2 2.9 fusion.17
  150.7 2.7 fusion.1
  153.5 2.8 fusion.16
  156.3 120.8 %all-gather.3.cloned.1.call-done = f32[24,3,256,256]{3,2,1,0:T(8,128)} async-done(((f32[3,3,256,256]{3,2,1,0:T(8,128)}), f32[24,3,256,256]{3,2,1,0:T(8,128)}) %all-gather.3.cloned.1.call-update) | async-done | bytes 18874384 | tf_op jit(solution)/shard_map/all_gather | solution.py:99
  277.0 9.3 %reduce_sum.9 = f32[3,3,256,256]{3,2,1,0:T(8,128)} reduce(f32[8,3,3,256,256]{4,3,2,1,0:T(8,128)} %bitcast.47, f32[]{:T(128)} %constant.66.clone.1), dimensions={0}, to_apply=%region_0.1 | reduce | flops 4128768 | bytes 21233668 | tf_op jit(solution)/shard_map/reduce_sum | solution.py:99
  287.7 10.5 %fusion.72 = f32[90,45,256]{2,1,0:T(8,128)S(1)} fusion(bf16[90,45,2304]{2,1,0:T(8,128)(2,1)} %fusion.16, bf16[2304,256,1]{1,0,2:T(8,128)(2,1)S(1)} %bitcast.52), kind=kOutput, calls=%fused_computation.114 | convolution fusion | flops 4777574400 | bytes 23989248 | tf_op jit(solution)/shard_map/dot_general | solution.py:88
  300.2 11.6 %convolution_convert_fusion = bf16[90,45,256]{2,1,0:T(8,128)(2,1)} fusion(bf16[90,45,2304]{2,1,0:T(8,128)(2,1)} %fusion.20, bf16[2304,256,1]{1,0,2:T(8,128)(2,1)S(1)} %bitcast.51), kind=kOutput, calls=%fused_computation.44 | convolution fusion | flops 4778611200 | bytes 21915648 | tf_op jit(solution)/shard_map/dot_general | solution.py:69
  311.8 45.9 %all-reduce.2.cloned.1.call-done = f32[3,3,256,256]{3,2,1,0:T(8,128)} async-done(((f32[3,3,256,256]{3,2,1,0:T(8,128)}), f32[3,3,256,256]{3,2,1,0:T(8,128)}) %all-reduce.2.cloned.1.call-update) | async-done | bytes 2359312 | tf_op jit(solution)/shard_map/psum | solution.py:101
  357.7 3.3 broadcast_multiply_fusion
  (62 shorter events, 28.1 us)
Async XLA Ops:
  7.2 269.9 %all-gather.3.cloned.1.call-start = ((), (), s32[]{:S(2)}) async-start(), calls=%async_computation.1 | async-start | bytes 21233664 | tf_op jit(solution)/shard_map/all_gather | solution.py:99
  8.0 5.7 %collective-permute-start = (bf16[1,45,256]{2,1,0:T(8,128)(2,1)S(1)}, bf16[1,45,256]{2,1,0:T(8,128)(2,1)S(1)}, u32[]{:S(2)}, u32[]{:S(2)}) collective-permute-start(bf16[1,45,256]{2,1,0:T(8,128)(2,1)S(1)} %get-tuple-element.38), channel_id=1, source_target_pairs={{0,8},{8,16},{16,24},{24,0},{1,9},{9,17},{17,25},{25,1},{2,10},{10... | collective-permute-start | bytes 69128 | tf_op jit(solution)/shard_map/ppermute | solution.py:15
  10.9 4.5 %collective-permute-start.1 = (bf16[1,45,256]{2,1,0:T(8,128)(2,1)S(1)}, bf16[1,45,256]{2,1,0:T(8,128)(2,1)S(1)}, u32[]{:S(2)}, u32[]{:S(2)}) collective-permute-start(bf16[1,45,256]{2,1,0:T(8,128)(2,1)S(1)} %get-tuple-element.37), channel_id=1, source_target_pairs={{8,0},{16,8},{24,16},{0,24},{9,1},{17,9},{25,17},{1,25},{10,2},{18... | collective-permute-start | bytes 69128 | tf_op jit(solution)/shard_map/ppermute | solution.py:17
  15.7 7.6 %collective-permute-start.2 = (bf16[92,1,256]{2,1,0:T(2,128)(2,1)S(1)}, bf16[92,1,256]{2,1,0:T(2,128)(2,1)S(1)}, u32[]{:S(2)}, u32[]{:S(2)}) collective-permute-start(bf16[92,1,256]{2,1,0:T(2,128)(2,1)S(1)} %get-tuple-element.33), channel_id=1, source_target_pairs={{0,1},{1,2},{2,3},{3,4},{4,5},{5,6},{6,7},{7,0},{8,9},{9,10},{10,1... | collective-permute-start | bytes 141320 | tf_op jit(solution)/shard_map/ppermute | solution.py:15
  15.7 7.5 %collective-permute-start.3 = (bf16[92,1,256]{2,1,0:T(2,128)(2,1)S(1)}, bf16[92,1,256]{2,1,0:T(2,128)(2,1)S(1)}, u32[]{:S(2)}, u32[]{:S(2)}) collective-permute-start(bf16[92,1,256]{2,1,0:T(2,128)(2,1)S(1)} %get-tuple-element.34), channel_id=1, source_target_pairs={{1,0},{2,1},{3,2},{4,3},{5,4},{6,5},{7,6},{0,7},{9,8},{10,9},{11,1... | collective-permute-start | bytes 141320 | tf_op jit(solution)/shard_map/ppermute | solution.py:17
  23.3 5.4 %collective-permute-start.4 = (bf16[2,47,256]{2,1,0:T(8,128)(2,1)S(1)}, bf16[2,47,256]{2,1,0:T(8,128)(2,1)S(1)}, u32[]{:S(2)}, u32[]{:S(2)}) collective-permute-start(bf16[2,47,256]{2,1,0:T(8,128)(2,1)S(1)} %fusion.54), channel_id=1, source_target_pairs={{0,4},{1,5},{2,6},{3,7},{4,0},{5,1},{6,2},{7,3},{8,12},{9,13},{10,... | collective-permute-start | bytes 144392 | tf_op jit(solution)/shard_map/ppermute | solution.py:27
  36.0 2.9 copy-start.1
  70.3 24.5 %copy-start.2 = (bf16[4050,256,1,1]{1,0,2,3:T(8,128)(2,1)S(1)}, bf16[4050,256,1,1]{1,0,2,3:T(8,128)(2,1)}, u32[]{:S(2)}) copy-start(bf16[4050,256,1,1]{1,0,2,3:T(8,128)(2,1)} %reshape.109) | copy-start | bytes 6220804
  105.1 2.9 copy-start.5
  105.1 252.6 %all-reduce.2.cloned.1.call-start = ((), (), s32[]{:S(2)}) async-start(), calls=%async_computation | async-start | bytes 4718592 | tf_op jit(solution)/shard_map/psum | solution.py:101
  106.0 8.8 %collective-permute-start.6 = (bf16[1,45,256]{2,1,0:T(8,128)(2,1)S(1)}, bf16[1,45,256]{2,1,0:T(8,128)(2,1)S(1)}, u32[]{:S(2)}, u32[]{:S(2)}) collective-permute-start(bf16[1,45,256]{2,1,0:T(8,128)(2,1)S(1)} %get-tuple-element.35), channel_id=1, source_target_pairs={{8,0},{16,8},{24,16},{0,24},{9,1},{17,9},{25,17},{1,25},{10,2},{18... | collective-permute-start | bytes 69128 | tf_op jit(solution)/shard_map/ppermute | solution.py:17
  107.9 4.7 %collective-permute-start.5 = (bf16[1,45,256]{2,1,0:T(8,128)(2,1)S(1)}, bf16[1,45,256]{2,1,0:T(8,128)(2,1)S(1)}, u32[]{:S(2)}, u32[]{:S(2)}) collective-permute-start(bf16[1,45,256]{2,1,0:T(8,128)(2,1)S(1)} %get-tuple-element.36), channel_id=1, source_target_pairs={{0,8},{8,16},{16,24},{24,0},{1,9},{9,17},{17,25},{25,1},{2,10},{10... | collective-permute-start | bytes 69128 | tf_op jit(solution)/shard_map/ppermute | solution.py:15
  115.7 9.1 %collective-permute-start.7 = (bf16[92,1,256]{2,1,0:T(2,128)(2,1)}, bf16[92,1,256]{2,1,0:T(2,128)(2,1)}, u32[]{:S(2)}, u32[]{:S(2)}) collective-permute-start(bf16[92,1,256]{2,1,0:T(2,128)(2,1)} %get-tuple-element.31), channel_id=1, source_target_pairs={{0,1},{1,2},{2,3},{3,4},{4,5},{5,6},{6,7},{7,0},{8,9},{9,10},{10,1... | collective-permute-start | bytes 141320 | tf_op jit(solution)/shard_map/ppermute | solution.py:15
  115.7 9.1 %collective-permute-start.8 = (bf16[92,1,256]{2,1,0:T(2,128)(2,1)}, bf16[92,1,256]{2,1,0:T(2,128)(2,1)S(1)}, u32[]{:S(2)}, u32[]{:S(2)}) collective-permute-start(bf16[92,1,256]{2,1,0:T(2,128)(2,1)} %get-tuple-element.32), channel_id=1, source_target_pairs={{1,0},{2,1},{3,2},{4,3},{5,4},{6,5},{7,6},{0,7},{9,8},{10,9},{11,1... | collective-permute-start | bytes 141320 | tf_op jit(solution)/shard_map/ppermute | solution.py:17
  125.4 172.7 %collective-permute-start.9 = (bf16[2,47,256]{2,1,0:T(8,128)(2,1)S(1)}, bf16[2,47,256]{2,1,0:T(8,128)(2,1)S(1)}, u32[]{:S(2)}, u32[]{:S(2)}) collective-permute-start(bf16[2,47,256]{2,1,0:T(8,128)(2,1)S(1)} %fusion.57), channel_id=1, source_target_pairs={{0,4},{1,5},{2,6},{3,7},{4,0},{5,1},{6,2},{7,3},{8,12},{9,13},{10,... | collective-permute-start | bytes 144392 | tf_op jit(solution)/shard_map/ppermute | solution.py:27
  141.0 3.6 copy-start
  286.4 1.3 copy-start.7
  287.7 10.5 %copy-start.4 = (bf16[1,3,256,256]{3,2,1,0:T(8,128)(2,1)S(1)}, bf16[1,3,256,256]{3,2,1,0:T(8,128)(2,1)}, u32[]{:S(2)}) copy-start(bf16[1,3,256,256]{3,2,1,0:T(8,128)(2,1)} %get-tuple-element.40) | copy-start | bytes 1179652
  287.7 10.7 %copy-start.3 = (bf16[1,3,256,256]{3,2,1,0:T(8,128)(2,1)S(1)}, bf16[1,3,256,256]{3,2,1,0:T(8,128)(2,1)}, u32[]{:S(2)}) copy-start(bf16[1,3,256,256]{3,2,1,0:T(8,128)(2,1)} %get-tuple-element.39) | copy-start | bytes 1179652
  298.6 1.6 copy-start.6
Sparse Core Ops, SparseCore 0:
  105.2 171.7 all-gather.2
  286.5 71.1 all-reduce.1
